TPU v7x, 128 devices: a whole 4x4x4 slice. The times are simulated.
128 devices in a mesh: layer: 4 (over x), node: 32 (over y, z, core).
Axes of the slice: x: 4, y: 4, z: 4, core: 2. Of those that a mesh axis runs over, the one named last changes fastest.
Arguments:
- features: bfloat16 [4, 8192, 512], P(None, 'node'), may hold values from -6 to 6
- w_self: bfloat16 [4, 512, 512], P('layer'), may hold values from -0.1875 to 0.1875
- w_neigh: bfloat16 [4, 512, 512], P('layer'), may hold values from -0.1875 to 0.1875
- w_out: bfloat16 [512, 172], replicated, may hold values from -0.25 to 0.25
- labels: int32 [4, 8192], P(None, 'node'), may hold values from 0 to 171
- train_mask: int32 [4, 8192], P(None, 'node'), may hold values 0 or 1
- tile_cols: int32 [4, 32, 2, 4], P(None, 'node'), may hold values from 0 to 3
- tile_vals: bfloat16 [4, 32, 2, 4, 128, 128], P(None, 'node'), may hold values from -0.25 to 0.25
- send_rows: int32 [4, 32, 32, 8], P(None, 'node'), may hold values from 0 to 255
- send_counts: int32 [4, 32, 32], P(None, 'node'), may hold values from 0 to 8, as said below
Outputs:
- layer_acts: bfloat16 [4, 4, 8192, 512], P('layer', None, 'node')
- act_grads: bfloat16 [4, 4, 8192, 512], P('layer', None, 'node')
- grad_self: float32 [4, 512, 512], P('layer')
- grad_neigh: float32 [4, 512, 512], P('layer')
Inputs may be any that keep to these rules, and one draw needn't show every extreme that they name: `send_counts`: in every span one partition, drawn per span, gets 8 rows from every partition, itself included; the other counts are at most 4. `send_rows`: entries of slots at or past the count are ignored; rows may repeat. `tile_cols`: A value below 2 is a tile of the partition's own rows; larger values are tiles of the received rows in source order, 8 slots per source, then zero rows; tiles of a row tile may repeat.
All inputs are finite; a program needn't handle non-finite values. No bound on the sum of `train_mask` on one device may be relied on, other than what follows from the above.
Results may differ from a plain program's by a relative error of at most 0.03.
Values may be sent and summed in bfloat16 or wider, within the bound.
No kernel may reach another device: no remote copies, remote signals or barrier semaphores. Data moves between devices by JAX's collectives and lax.ppermute only.
A program may use at most 128 MiB of HBM per device.

v0:
```python
import jax
import jax.numpy as jnp
from jax import lax
from jax.sharding import PartitionSpec as P


def from_behind(value, axis, steps):
    count = lax.axis_size(axis)
    first, last = (max(0, -steps), min(count, count - steps))
    return lax.ppermute(value, axis, [(source, source + steps) for source in range(first, last)])


def silu_slope(preact):
    sigma = jax.nn.sigmoid(preact)
    return sigma * (1.0 + preact * (1.0 - sigma))


def pick(array, index):
    return lax.dynamic_index_in_dim(array, index, 0, keepdims=False)


def put_row(buffer, value, index, valid):
    current = pick(buffer, index)
    return lax.dynamic_update_index_in_dim(buffer, jnp.where(valid, value, current), index, 0)


def live_slots(send_list, counts):
    return jnp.arange(send_list.shape[1])[None, :] < counts[:, None]


def layer_forward(hidden_in, weight_self, weight_neigh, col_tiles, values, send_list, counts):
    feat_dim = hidden_in.shape[1]
    tile_size = values.shape[-1]
    is_live = live_slots(send_list, counts)
    outgoing = jnp.where(
        is_live[:, :, None], jnp.take(hidden_in, send_list, axis=0), jnp.zeros((), hidden_in.dtype)
    )
    arrived = lax.all_to_all(outgoing, "node", split_axis=0, concat_axis=0, tiled=True)
    extended = jnp.concatenate([hidden_in, arrived.reshape(-1, feat_dim)], axis=0)
    blocks = jnp.take(extended.reshape(-1, tile_size, feat_dim), col_tiles, axis=0)
    summed = jnp.einsum("rkij,rkjd->rid", values, blocks, preferred_element_type=jnp.float32)
    aggregate = summed.reshape(hidden_in.shape).astype(jnp.bfloat16)
    preact = jnp.dot(hidden_in, weight_self, preferred_element_type=jnp.float32)
    preact = preact + jnp.dot(aggregate, weight_neigh, preferred_element_type=jnp.float32)
    return (aggregate, preact, jax.nn.silu(preact).astype(jnp.bfloat16))


def layer_backward(
    d_out,
    hidden_in,
    aggregate,
    preact,
    weight_self,
    weight_neigh,
    col_tiles,
    values,
    send_list,
    counts,
):
    node_rows, feat_dim = hidden_in.shape
    row_tiles, degree, tile_size = (values.shape[0], values.shape[1], values.shape[-1])
    peers, slot_count = send_list.shape
    d_pre = (d_out.astype(jnp.float32) * silu_slope(preact)).astype(jnp.bfloat16)
    over_rows = (((0,), (0,)), ((), ()))
    over_cols = (((1,), (1,)), ((), ()))
    g_self = lax.dot_general(hidden_in, d_pre, over_rows, preferred_element_type=jnp.float32)
    g_neigh = lax.dot_general(aggregate, d_pre, over_rows, preferred_element_type=jnp.float32)
    back_self = lax.dot_general(d_pre, weight_self, over_cols, preferred_element_type=jnp.float32)
    d_agg = lax.dot_general(
        d_pre, weight_neigh, over_cols, preferred_element_type=jnp.float32
    ).astype(jnp.bfloat16)
    pieces = jnp.einsum(
        "rkij,rid->rkjd",
        values,
        d_agg.reshape(row_tiles, tile_size, feat_dim),
        preferred_element_type=jnp.float32,
    )
    col_count = (node_rows + peers * slot_count + tile_size - 1) // tile_size
    selector = (col_tiles.reshape(-1)[None, :] == jnp.arange(col_count)[:, None]).astype(
        jnp.float32
    )
    d_ext = jnp.einsum(
        "cn,njd->cjd",
        selector,
        pieces.reshape(row_tiles * degree, tile_size, feat_dim),
        precision=lax.Precision.HIGHEST,
    )
    d_ext = d_ext.reshape(-1, feat_dim)
    local_part = d_ext[:node_rows]
    remote = (
        d_ext[node_rows : node_rows + peers * slot_count]
        .reshape(peers, slot_count, feat_dim)
        .astype(jnp.bfloat16)
    )
    returned = lax.all_to_all(remote, "node", split_axis=0, concat_axis=0, tiled=True)
    is_live = live_slots(send_list, counts)
    masked = jnp.where(
        is_live[:, :, None], returned.astype(jnp.float32), jnp.zeros((), jnp.float32)
    )
    scattered = jax.ops.segment_sum(
        masked.reshape(-1, feat_dim), send_list.reshape(-1), num_segments=node_rows
    )
    d_in = (back_self + local_part + scattered).astype(jnp.bfloat16)
    return (d_in, g_self, g_neigh)


def finish_grads(grad_pair, scale):
    summed = (
        lax.psum(grad_pair[0].astype(jnp.bfloat16), "node").astype(jnp.float32),
        lax.psum(grad_pair[1].astype(jnp.bfloat16), "node").astype(jnp.float32),
    )
    return (summed[0] * scale, summed[1] * scale)


def body(
    features,
    w_self,
    w_neigh,
    w_out,
    labels,
    train_mask,
    tile_cols,
    tile_vals,
    send_rows,
    send_counts,
):
    my_section = lax.axis_index("layer")
    sections = lax.axis_size("layer")
    spans, node_rows, feat_dim = features.shape
    classes = w_out.shape[1]
    scale = 1.0 / (spans * node_rows * lax.axis_size("node"))

    def graph_of(span_idx):
        return (
            pick(tile_cols, span_idx)[0],
            pick(tile_vals, span_idx)[0],
            pick(send_rows, span_idx)[0],
            pick(send_counts, span_idx)[0],
        )

    rows_zero = jnp.zeros((node_rows, feat_dim), jnp.bfloat16)
    block_bf = jnp.zeros((spans, node_rows, feat_dim), jnp.bfloat16)
    block_f32 = jnp.zeros((spans, node_rows, feat_dim), jnp.float32)
    square_zero = jnp.zeros((feat_dim, feat_dim), jnp.float32)
    weight_self = w_self[0]
    weight_neigh = w_neigh[0]
    steps_total = spans + sections - 1

    def forward_step(step, carry):
        incoming, saved_in, saved_agg, saved_pre, acts = carry
        span_idx = step - my_section
        valid = (span_idx >= 0) & (span_idx < spans)
        safe_idx = jnp.clip(span_idx, 0, spans - 1)
        hidden_in = jnp.where(my_section == 0, pick(features, safe_idx), incoming)
        aggregate, preact, hidden_out = layer_forward(
            hidden_in, weight_self, weight_neigh, *graph_of(safe_idx)
        )
        saved_in = put_row(saved_in, hidden_in, safe_idx, valid)
        saved_agg = put_row(saved_agg, aggregate, safe_idx, valid)
        saved_pre = put_row(saved_pre, preact, safe_idx, valid)
        acts = put_row(acts, hidden_out, safe_idx, valid)
        outgoing = from_behind(hidden_out, "layer", 1)
        return (outgoing, saved_in, saved_agg, saved_pre, acts)

    start = (rows_zero, block_bf, block_bf, block_f32, block_bf)
    fwd_done = lax.fori_loop(0, steps_total, forward_step, start)
    saved_in, saved_agg, saved_pre, acts = (fwd_done[1], fwd_done[2], fwd_done[3], fwd_done[4])
    logits = jnp.einsum("...d,dc->...c", acts, w_out, preferred_element_type=jnp.float32)
    expo = jnp.exp(logits)
    probs = expo / jnp.sum(expo, axis=-1, keepdims=True)
    onehot = (labels[..., None] == jnp.arange(classes)).astype(jnp.float32)
    g_logits = (train_mask[..., None].astype(jnp.float32) * (probs - onehot)).astype(jnp.bfloat16)
    d_top = jnp.einsum("...c,dc->...d", g_logits, w_out, preferred_element_type=jnp.float32).astype(
        jnp.bfloat16
    )

    def backward_step(step, carry):
        incoming, sum_self, sum_neigh, grads_out = carry
        span_idx = step - (sections - 1 - my_section)
        valid = (span_idx >= 0) & (span_idx < spans)
        safe_idx = jnp.clip(span_idx, 0, spans - 1)
        d_out = jnp.where(my_section == sections - 1, pick(d_top, safe_idx), incoming)
        hidden_in = pick(saved_in, safe_idx)
        graph = graph_of(safe_idx)
        aggregate = pick(saved_agg, safe_idx)
        preact = pick(saved_pre, safe_idx)
        d_in, g_self, g_neigh = layer_backward(
            d_out, hidden_in, aggregate, preact, weight_self, weight_neigh, *graph
        )
        sum_self = sum_self + jnp.where(valid, g_self, 0.0)
        sum_neigh = sum_neigh + jnp.where(valid, g_neigh, 0.0)
        grads_out = put_row(grads_out, d_in, safe_idx, valid)
        outgoing = from_behind(d_in, "layer", -1)
        return (outgoing, sum_self, sum_neigh, grads_out)

    bwd_done = lax.fori_loop(
        0, steps_total, backward_step, (rows_zero, square_zero, square_zero, block_bf)
    )
    grad_self, grad_neigh = finish_grads((bwd_done[1][None], bwd_done[2][None]), scale)
    return (acts[None], bwd_done[3][None], grad_self, grad_neigh)


def solution(mesh):
    in_specs = (
        P(None, "node", None),
        P("layer", None, None),
        P("layer", None, None),
        P(),
        P(None, "node"),
        P(None, "node"),
        P(None, "node", None, None),
        P(None, "node", None, None, None, None),
        P(None, "node", None, None),
        P(None, "node", None),
    )
    out_specs = (
        P("layer", None, "node", None),
        P("layer", None, "node", None),
        P("layer", None, None),
        P("layer", None, None),
    )
    return jax.shard_map(body, mesh=mesh, in_specs=in_specs, out_specs=out_specs, check_vma=False)
```

profile of v0, /device:TPU:1, one launch (start us, length us, event | category | flops | bytes accessed | tf_op | source)
XLA Modules:
  0.0 613.9 jit_solution(9725740799689017812)
XLA Ops:
  12.6 233.1 %while.44 = (s32[]{:T(128)}, bf16[256,512]{1,0:T(8,128)(2,1)S(1)}, bf16[4,256,512]{2,1,0:T(8,128)(2,1)}, bf16[4,256,512]{2,1,0:T(8,128)(2,1)}, f32[4,256,512]{2,...) while((s32[]{:T(128)}, bf16[256,512]{1,0:T(8,128)(2,1)S(1)}, ...), condition=%wide.region_1.2_spmd, body=%wide.region_0.1_spmd.sunk | while | flops 406065728 | bytes 27805224 | solution.py:166
  17.8 9.6 %all-to-all-start = ((bf16[32,8,512]{2,1,0:T(8,128)(2,1)}), bf16[32,8,512]{2,1,0:T(8,128)(2,1)S(1)}, u32[]{:S(2)}, u32[]{:S(2)}) async-start(bf16[32,8,512]{2,1,0:T(8,128)(2,1)} %fusion.105), calls=%async_computation | async-start | bytes 524288 | tf_op jit(solution)/shard_map/while/body/eval_jaxpr/all_to_all | solution.py:38
  29.8 6.6 %all-to-all-done = bf16[32,8,512]{2,1,0:T(8,128)(2,1)S(1)} async-done(((bf16[32,8,512]{2,1,0:T(8,128)(2,1)}), bf16[32,8,512]{2,1,0:T(8,128)(2,1)S(1)}, u32[]{:S(2)}, u32[]{:S(2)}) %all-to-all-start) | async-done | bytes 262176 | tf_op jit(solution)/shard_map/while/body/eval_jaxpr/all_to_all | solution.py:38
  61.4 6.8 %all-to-all-done = bf16[32,8,512]{2,1,0:T(8,128)(2,1)S(1)} async-done(((bf16[32,8,512]{2,1,0:T(8,128)(2,1)}), bf16[32,8,512]{2,1,0:T(8,128)(2,1)S(1)}, u32[]{:S(2)}, u32[]{:S(2)}) %all-to-all-start) | async-done | bytes 262176 | tf_op jit(solution)/shard_map/while/body/eval_jaxpr/all_to_all | solution.py:38
  94.1 6.8 %all-to-all-done = bf16[32,8,512]{2,1,0:T(8,128)(2,1)S(1)} async-done(((bf16[32,8,512]{2,1,0:T(8,128)(2,1)}), bf16[32,8,512]{2,1,0:T(8,128)(2,1)S(1)}, u32[]{:S(2)}, u32[]{:S(2)}) %all-to-all-start) | async-done | bytes 262176 | tf_op jit(solution)/shard_map/while/body/eval_jaxpr/all_to_all | solution.py:38
  126.8 6.8 %all-to-all-done = bf16[32,8,512]{2,1,0:T(8,128)(2,1)S(1)} async-done(((bf16[32,8,512]{2,1,0:T(8,128)(2,1)}), bf16[32,8,512]{2,1,0:T(8,128)(2,1)S(1)}, u32[]{:S(2)}, u32[]{:S(2)}) %all-to-all-start) | async-done | bytes 262176 | tf_op jit(solution)/shard_map/while/body/eval_jaxpr/all_to_all | solution.py:38
  159.5 6.8 %all-to-all-done = bf16[32,8,512]{2,1,0:T(8,128)(2,1)S(1)} async-done(((bf16[32,8,512]{2,1,0:T(8,128)(2,1)}), bf16[32,8,512]{2,1,0:T(8,128)(2,1)S(1)}, u32[]{:S(2)}, u32[]{:S(2)}) %all-to-all-start) | async-done | bytes 262176 | tf_op jit(solution)/shard_map/while/body/eval_jaxpr/all_to_all | solution.py:38
  192.2 6.8 %all-to-all-done = bf16[32,8,512]{2,1,0:T(8,128)(2,1)S(1)} async-done(((bf16[32,8,512]{2,1,0:T(8,128)(2,1)}), bf16[32,8,512]{2,1,0:T(8,128)(2,1)S(1)}, u32[]{:S(2)}, u32[]{:S(2)}) %all-to-all-start) | async-done | bytes 262176 | tf_op jit(solution)/shard_map/while/body/eval_jaxpr/all_to_all | solution.py:38
  224.9 6.8 %all-to-all-done = bf16[32,8,512]{2,1,0:T(8,128)(2,1)S(1)} async-done(((bf16[32,8,512]{2,1,0:T(8,128)(2,1)}), bf16[32,8,512]{2,1,0:T(8,128)(2,1)S(1)}, u32[]{:S(2)}, u32[]{:S(2)}) %all-to-all-start) | async-done | bytes 262176 | tf_op jit(solution)/shard_map/while/body/eval_jaxpr/all_to_all | solution.py:38
  249.5 247.1 %while.45 = (s32[]{:T(128)}, bf16[256,512]{1,0:T(8,128)(2,1)}, f32[512,512]{1,0:T(8,128)}, f32[512,512]{1,0:T(8,128)}, bf16[4,256,512]{2,1,0:T(8,128)(2,1)}, /*i...) while((s32[]{:T(128)}, bf16[256,512]{1,0:T(8,128)(2,1)}, ...), condition=%wide.region_5.6_spmd.clone, body=%wide.region_3.5_spmd.clone.sunk | while | flops 700186880 | bytes 31204564 | solution.py:196
  257.0 5.2 all-to-all-start.1
  277.6 8.1 %collective-permute-done.1 = bf16[256,512]{1,0:T(8,128)(2,1)} collective-permute-done((bf16[256,512]{1,0:T(8,128)(2,1)S(1)}, bf16[256,512]{1,0:T(8,128)(2,1)}, u32[]{:S(2)}, u32[]{:S(2)}) %collective-permute-start.1) | collective-permute-done | bytes 262176 | tf_op jit(solution)/shard_map/while/body/eval_jaxpr/ppermute | solution.py:10
  313.6 7.1 %collective-permute-done.1 = bf16[256,512]{1,0:T(8,128)(2,1)} collective-permute-done((bf16[256,512]{1,0:T(8,128)(2,1)S(1)}, bf16[256,512]{1,0:T(8,128)(2,1)}, u32[]{:S(2)}, u32[]{:S(2)}) %collective-permute-start.1) | collective-permute-done | bytes 262176 | tf_op jit(solution)/shard_map/while/body/eval_jaxpr/ppermute | solution.py:10
  328.2 5.2 all-to-all-start.1
  348.8 7.1 %collective-permute-done.1 = bf16[256,512]{1,0:T(8,128)(2,1)} collective-permute-done((bf16[256,512]{1,0:T(8,128)(2,1)S(1)}, bf16[256,512]{1,0:T(8,128)(2,1)}, u32[]{:S(2)}, u32[]{:S(2)}) %collective-permute-start.1) | collective-permute-done | bytes 262176 | tf_op jit(solution)/shard_map/while/body/eval_jaxpr/ppermute | solution.py:10
  363.4 5.2 all-to-all-start.1
  383.9 7.1 %collective-permute-done.1 = bf16[256,512]{1,0:T(8,128)(2,1)} collective-permute-done((bf16[256,512]{1,0:T(8,128)(2,1)S(1)}, bf16[256,512]{1,0:T(8,128)(2,1)}, u32[]{:S(2)}, u32[]{:S(2)}) %collective-permute-start.1) | collective-permute-done | bytes 262176 | tf_op jit(solution)/shard_map/while/body/eval_jaxpr/ppermute | solution.py:10
  398.5 5.2 all-to-all-start.1
  419.1 7.1 %collective-permute-done.1 = bf16[256,512]{1,0:T(8,128)(2,1)} collective-permute-done((bf16[256,512]{1,0:T(8,128)(2,1)S(1)}, bf16[256,512]{1,0:T(8,128)(2,1)}, u32[]{:S(2)}, u32[]{:S(2)}) %collective-permute-start.1) | collective-permute-done | bytes 262176 | tf_op jit(solution)/shard_map/while/body/eval_jaxpr/ppermute | solution.py:10
  433.7 5.2 all-to-all-start.1
  454.3 7.1 %collective-permute-done.1 = bf16[256,512]{1,0:T(8,128)(2,1)} collective-permute-done((bf16[256,512]{1,0:T(8,128)(2,1)S(1)}, bf16[256,512]{1,0:T(8,128)(2,1)}, u32[]{:S(2)}, u32[]{:S(2)}) %collective-permute-start.1) | collective-permute-done | bytes 262176 | tf_op jit(solution)/shard_map/while/body/eval_jaxpr/ppermute | solution.py:10
  468.9 5.2 all-to-all-start.1
  489.5 7.1 %collective-permute-done.1 = bf16[256,512]{1,0:T(8,128)(2,1)} collective-permute-done((bf16[256,512]{1,0:T(8,128)(2,1)S(1)}, bf16[256,512]{1,0:T(8,128)(2,1)}, u32[]{:S(2)}, u32[]{:S(2)}) %collective-permute-start.1) | collective-permute-done | bytes 262176 | tf_op jit(solution)/shard_map/while/body/eval_jaxpr/ppermute | solution.py:10
  499.2 103.5 %all-reduce.3.cloned.1.call-done = (bf16[1,512,512]{2,1,0:T(8,128)(2,1)}, bf16[1,512,512]{2,1,0:T(8,128)(2,1)}) async-done(((bf16[1,512,512]{2,1,0:T(8,128)(2,1)}, bf16[1,512,512]{2,1,0:T(8,128)(2,1)}), (bf16[1,512,512]{2,1,0:T(8,128)(2,1)}, bf16[1,512,512]{2,1,0:T(8,128)(2,1)})) %all-reduce.3.cloned.1.call-update) | async-done | bytes 1048592 | tf_op jit(solution)/shard_map/psum | solution.py:109
  (429 shorter events, 356.2 us)
Async XLA Ops:
  7.2 595.6 %all-reduce.3.cloned.1.call-start = ((), (), s32[]{:S(2)}) async-start(), calls=%async_computation.2 | async-start | bytes 2097152 | tf_op jit(solution)/shard_map/psum | solution.py:109
  17.8 18.6 %all-to-all-start = ((bf16[32,8,512]{2,1,0:T(8,128)(2,1)}), bf16[32,8,512]{2,1,0:T(8,128)(2,1)S(1)}, u32[]{:S(2)}, u32[]{:S(2)}) async-start(bf16[32,8,512]{2,1,0:T(8,128)(2,1)} %fusion.105), calls=%async_computation | async-start | bytes 524288 | tf_op jit(solution)/shard_map/while/body/eval_jaxpr/all_to_all | solution.py:38
  54.5 13.6 %all-to-all-start = ((bf16[32,8,512]{2,1,0:T(8,128)(2,1)}), bf16[32,8,512]{2,1,0:T(8,128)(2,1)S(1)}, u32[]{:S(2)}, u32[]{:S(2)}) async-start(bf16[32,8,512]{2,1,0:T(8,128)(2,1)} %fusion.105), calls=%async_computation | async-start | bytes 524288 | tf_op jit(solution)/shard_map/while/body/eval_jaxpr/all_to_all | solution.py:38
  72.4 9.7 %collective-permute-start = (bf16[256,512]{1,0:T(8,128)(2,1)S(1)}, bf16[256,512]{1,0:T(8,128)(2,1)S(1)}, u32[]{:S(2)}, u32[]{:S(2)}) collective-permute-start(bf16[256,512]{1,0:T(8,128)(2,1)S(1)} %get-tuple-element.1054), channel_id=1, source_target_pairs={{0,32},{32,64},{64,96},{1,33},{33,65},{65,97},{2,34},{34,66},{66,9... | collective-permute-start | bytes 786440 | tf_op jit(solution)/shard_map/while/body/eval_jaxpr/ppermute | solution.py:10
  87.2 13.6 %all-to-all-start = ((bf16[32,8,512]{2,1,0:T(8,128)(2,1)}), bf16[32,8,512]{2,1,0:T(8,128)(2,1)S(1)}, u32[]{:S(2)}, u32[]{:S(2)}) async-start(bf16[32,8,512]{2,1,0:T(8,128)(2,1)} %fusion.105), calls=%async_computation | async-start | bytes 524288 | tf_op jit(solution)/shard_map/while/body/eval_jaxpr/all_to_all | solution.py:38
  105.1 9.7 %collective-permute-start = (bf16[256,512]{1,0:T(8,128)(2,1)S(1)}, bf16[256,512]{1,0:T(8,128)(2,1)S(1)}, u32[]{:S(2)}, u32[]{:S(2)}) collective-permute-start(bf16[256,512]{1,0:T(8,128)(2,1)S(1)} %get-tuple-element.1054), channel_id=1, source_target_pairs={{0,32},{32,64},{64,96},{1,33},{33,65},{65,97},{2,34},{34,66},{66,9... | collective-permute-start | bytes 786440 | tf_op jit(solution)/shard_map/while/body/eval_jaxpr/ppermute | solution.py:10
  119.9 13.6 %all-to-all-start = ((bf16[32,8,512]{2,1,0:T(8,128)(2,1)}), bf16[32,8,512]{2,1,0:T(8,128)(2,1)S(1)}, u32[]{:S(2)}, u32[]{:S(2)}) async-start(bf16[32,8,512]{2,1,0:T(8,128)(2,1)} %fusion.105), calls=%async_computation | async-start | bytes 524288 | tf_op jit(solution)/shard_map/while/body/eval_jaxpr/all_to_all | solution.py:38
  137.8 9.7 %collective-permute-start = (bf16[256,512]{1,0:T(8,128)(2,1)S(1)}, bf16[256,512]{1,0:T(8,128)(2,1)S(1)}, u32[]{:S(2)}, u32[]{:S(2)}) collective-permute-start(bf16[256,512]{1,0:T(8,128)(2,1)S(1)} %get-tuple-element.1054), channel_id=1, source_target_pairs={{0,32},{32,64},{64,96},{1,33},{33,65},{65,97},{2,34},{34,66},{66,9... | collective-permute-start | bytes 786440 | tf_op jit(solution)/shard_map/while/body/eval_jaxpr/ppermute | solution.py:10
  152.6 13.6 %all-to-all-start = ((bf16[32,8,512]{2,1,0:T(8,128)(2,1)}), bf16[32,8,512]{2,1,0:T(8,128)(2,1)S(1)}, u32[]{:S(2)}, u32[]{:S(2)}) async-start(bf16[32,8,512]{2,1,0:T(8,128)(2,1)} %fusion.105), calls=%async_computation | async-start | bytes 524288 | tf_op jit(solution)/shard_map/while/body/eval_jaxpr/all_to_all | solution.py:38
  170.5 9.7 %collective-permute-start = (bf16[256,512]{1,0:T(8,128)(2,1)S(1)}, bf16[256,512]{1,0:T(8,128)(2,1)S(1)}, u32[]{:S(2)}, u32[]{:S(2)}) collective-permute-start(bf16[256,512]{1,0:T(8,128)(2,1)S(1)} %get-tuple-element.1054), channel_id=1, source_target_pairs={{0,32},{32,64},{64,96},{1,33},{33,65},{65,97},{2,34},{34,66},{66,9... | collective-permute-start | bytes 786440 | tf_op jit(solution)/shard_map/while/body/eval_jaxpr/ppermute | solution.py:10
  185.4 13.6 %all-to-all-start = ((bf16[32,8,512]{2,1,0:T(8,128)(2,1)}), bf16[32,8,512]{2,1,0:T(8,128)(2,1)S(1)}, u32[]{:S(2)}, u32[]{:S(2)}) async-start(bf16[32,8,512]{2,1,0:T(8,128)(2,1)} %fusion.105), calls=%async_computation | async-start | bytes 524288 | tf_op jit(solution)/shard_map/while/body/eval_jaxpr/all_to_all | solution.py:38
  203.2 9.7 %collective-permute-start = (bf16[256,512]{1,0:T(8,128)(2,1)S(1)}, bf16[256,512]{1,0:T(8,128)(2,1)S(1)}, u32[]{:S(2)}, u32[]{:S(2)}) collective-permute-start(bf16[256,512]{1,0:T(8,128)(2,1)S(1)} %get-tuple-element.1054), channel_id=1, source_target_pairs={{0,32},{32,64},{64,96},{1,33},{33,65},{65,97},{2,34},{34,66},{66,9... | collective-permute-start | bytes 786440 | tf_op jit(solution)/shard_map/while/body/eval_jaxpr/ppermute | solution.py:10
  218.1 13.6 %all-to-all-start = ((bf16[32,8,512]{2,1,0:T(8,128)(2,1)}), bf16[32,8,512]{2,1,0:T(8,128)(2,1)S(1)}, u32[]{:S(2)}, u32[]{:S(2)}) async-start(bf16[32,8,512]{2,1,0:T(8,128)(2,1)} %fusion.105), calls=%async_computation | async-start | bytes 524288 | tf_op jit(solution)/shard_map/while/body/eval_jaxpr/all_to_all | solution.py:38
  235.9 9.7 %collective-permute-start = (bf16[256,512]{1,0:T(8,128)(2,1)S(1)}, bf16[256,512]{1,0:T(8,128)(2,1)S(1)}, u32[]{:S(2)}, u32[]{:S(2)}) collective-permute-start(bf16[256,512]{1,0:T(8,128)(2,1)S(1)} %get-tuple-element.1054), channel_id=1, source_target_pairs={{0,32},{32,64},{64,96},{1,33},{33,65},{65,97},{2,34},{34,66},{66,9... | collective-permute-start | bytes 786440 | tf_op jit(solution)/shard_map/while/body/eval_jaxpr/ppermute | solution.py:10
  257.0 14.3 %all-to-all-start.1 = ((bf16[32,8,512]{2,1,0:T(8,128)(2,1)}), bf16[32,8,512]{2,1,0:T(8,128)(2,1)}, u32[]{:S(2)}, u32[]{:S(2)}) async-start(bf16[32,8,512]{2,1,0:T(8,128)(2,1)} %bitcast.226), calls=%async_computation.1 | async-start | bytes 524288 | tf_op jit(solution)/shard_map/while/body/eval_jaxpr/all_to_all | solution.py:95
  275.0 10.8 %collective-permute-start.1 = (bf16[256,512]{1,0:T(8,128)(2,1)S(1)}, bf16[256,512]{1,0:T(8,128)(2,1)}, u32[]{:S(2)}, u32[]{:S(2)}) collective-permute-start(bf16[256,512]{1,0:T(8,128)(2,1)S(1)} %get-tuple-element.1075), channel_id=1, source_target_pairs={{32,0},{64,32},{96,64},{33,1},{65,33},{97,65},{34,2},{66,34},{98,6... | collective-permute-start | bytes 786440 | tf_op jit(solution)/shard_map/while/body/eval_jaxpr/ppermute | solution.py:10
  293.3 14.0 %all-to-all-start.1 = ((bf16[32,8,512]{2,1,0:T(8,128)(2,1)}), bf16[32,8,512]{2,1,0:T(8,128)(2,1)}, u32[]{:S(2)}, u32[]{:S(2)}) async-start(bf16[32,8,512]{2,1,0:T(8,128)(2,1)} %bitcast.226), calls=%async_computation.1 | async-start | bytes 524288 | tf_op jit(solution)/shard_map/while/body/eval_jaxpr/all_to_all | solution.py:95
  310.9 9.7 %collective-permute-start.1 = (bf16[256,512]{1,0:T(8,128)(2,1)S(1)}, bf16[256,512]{1,0:T(8,128)(2,1)}, u32[]{:S(2)}, u32[]{:S(2)}) collective-permute-start(bf16[256,512]{1,0:T(8,128)(2,1)S(1)} %get-tuple-element.1075), channel_id=1, source_target_pairs={{32,0},{64,32},{96,64},{33,1},{65,33},{97,65},{34,2},{66,34},{98,6... | collective-permute-start | bytes 786440 | tf_op jit(solution)/shard_map/while/body/eval_jaxpr/ppermute | solution.py:10
  328.2 14.3 %all-to-all-start.1 = ((bf16[32,8,512]{2,1,0:T(8,128)(2,1)}), bf16[32,8,512]{2,1,0:T(8,128)(2,1)}, u32[]{:S(2)}, u32[]{:S(2)}) async-start(bf16[32,8,512]{2,1,0:T(8,128)(2,1)} %bitcast.226), calls=%async_computation.1 | async-start | bytes 524288 | tf_op jit(solution)/shard_map/while/body/eval_jaxpr/all_to_all | solution.py:95
  346.1 9.7 %collective-permute-start.1 = (bf16[256,512]{1,0:T(8,128)(2,1)S(1)}, bf16[256,512]{1,0:T(8,128)(2,1)}, u32[]{:S(2)}, u32[]{:S(2)}) collective-permute-start(bf16[256,512]{1,0:T(8,128)(2,1)S(1)} %get-tuple-element.1075), channel_id=1, source_target_pairs={{32,0},{64,32},{96,64},{33,1},{65,33},{97,65},{34,2},{66,34},{98,6... | collective-permute-start | bytes 786440 | tf_op jit(solution)/shard_map/while/body/eval_jaxpr/ppermute | solution.py:10
  363.4 14.3 %all-to-all-start.1 = ((bf16[32,8,512]{2,1,0:T(8,128)(2,1)}), bf16[32,8,512]{2,1,0:T(8,128)(2,1)}, u32[]{:S(2)}, u32[]{:S(2)}) async-start(bf16[32,8,512]{2,1,0:T(8,128)(2,1)} %bitcast.226), calls=%async_computation.1 | async-start | bytes 524288 | tf_op jit(solution)/shard_map/while/body/eval_jaxpr/all_to_all | solution.py:95
  398.5 14.3 %all-to-all-start.1 = ((bf16[32,8,512]{2,1,0:T(8,128)(2,1)}), bf16[32,8,512]{2,1,0:T(8,128)(2,1)}, u32[]{:S(2)}, u32[]{:S(2)}) async-start(bf16[32,8,512]{2,1,0:T(8,128)(2,1)} %bitcast.226), calls=%async_computation.1 | async-start | bytes 524288 | tf_op jit(solution)/shard_map/while/body/eval_jaxpr/all_to_all | solution.py:95
  433.7 14.3 %all-to-all-start.1 = ((bf16[32,8,512]{2,1,0:T(8,128)(2,1)}), bf16[32,8,512]{2,1,0:T(8,128)(2,1)}, u32[]{:S(2)}, u32[]{:S(2)}) async-start(bf16[32,8,512]{2,1,0:T(8,128)(2,1)} %bitcast.226), calls=%async_computation.1 | async-start | bytes 524288 | tf_op jit(solution)/shard_map/while/body/eval_jaxpr/all_to_all | solution.py:95
  468.9 14.3 %all-to-all-start.1 = ((bf16[32,8,512]{2,1,0:T(8,128)(2,1)}), bf16[32,8,512]{2,1,0:T(8,128)(2,1)}, u32[]{:S(2)}, u32[]{:S(2)}) async-start(bf16[32,8,512]{2,1,0:T(8,128)(2,1)} %bitcast.226), calls=%async_computation.1 | async-start | bytes 524288 | tf_op jit(solution)/shard_map/while/body/eval_jaxpr/all_to_all | solution.py:95
  (46 other events, 799.4 us)
Sparse Core Ops, SparseCore 0:
  499.4 103.3 all-reduce.2
where the time goes:
time: 619 us; the launch traced here: 614 us
  waiting for transfers between devices  254 us (41%)
  starting transfers between devices  110 us (18%)
  matrix products  99.4 us (16%)
  other arithmetic  80.9 us (13%)
  local copies, waits for them, and re-layouts  53 us (9%)
  between operations  14.1 us (2%)
    psum x1, waiting for transfers between devices, finish_grads(): lax.psum(grad_pair[0].astype(jnp.bfloat16), 'node').astype(jnp.float32)  103 us
    ppermute x14, waiting for transfers between devices, from_behind(): lax.ppermute(value, axis, [(source, source + steps) for source in range(f...  70.6 us
    all_to_all x7, waiting for transfers between devices, layer_forward(): lax.all_to_all(outgoing, 'node', split_axis=0, concat_axis=0, tiled=True)  47.2 us
    ppermute x14, starting transfers between devices, from_behind(): lax.ppermute(value, axis, [(source, source + steps) for source in range(f...  37.7 us
    all_to_all x7, starting transfers between devices, layer_forward(): lax.all_to_all(outgoing, 'node', split_axis=0, concat_axis=0, tiled=True)  36.7 us
    dynamic_update_slice x28, other arithmetic, put_row(): lax.dynamic_update_index_in_dim(buffer, jnp.where(valid, value, current),...  36.2 us
    all_to_all x7, starting transfers between devices, layer_backward(): lax.all_to_all(remote, 'node', split_axis=0, concat_axis=0, tiled=True)  35.8 us
    all_to_all x7, waiting for transfers between devices, layer_backward(): lax.all_to_all(remote, 'node', split_axis=0, concat_axis=0, tiled=True)  33.1 us
  transfers between devices with their start and end apart: 29, of which 29 were waited for; matrix products, arithmetic and copies ran while one was open for 12% of the time, Pallas kernels for 0%

commit v1 on v0

--- a/solution.py
+++ b/solution.py
@@ -2,6 +2,12 @@
 import jax.numpy as jnp
 from jax import lax
 from jax.sharding import PartitionSpec as P
+
+
+def add_all(value, mesh_axis):
+    blocks = lax.all_gather(value, mesh_axis, axis=0, tiled=False)
+    total = blocks.sum(axis=0)
+    return total
 
 
 def from_behind(value, axis, steps):
@@ -106,7 +112,7 @@
 
 def finish_grads(grad_pair, scale):
     summed = (
-        lax.psum(grad_pair[0].astype(jnp.bfloat16), "node").astype(jnp.float32),
+        add_all(grad_pair[0].astype(jnp.bfloat16), "node").astype(jnp.float32),
         lax.psum(grad_pair[1].astype(jnp.bfloat16), "node").astype(jnp.float32),
     )
     return (summed[0] * scale, summed[1] * scale)

time: 619 us -> 698 us (1.13)
  waiting for transfers between devices: 254 us -> 326 us
  other arithmetic: 80.9 us -> 89.1 us
    all_gather x0 -> x1, waiting for transfers between devices: none -> 73.5 us  [add_all(): blocks = lax.all_gather(value, mesh_axis, axis=0, tiled=False)]
    reduce_sum x0 -> x1, other arithmetic: none -> 8.8 us  [add_all(): total = blocks.sum(axis=0)]
    dot_general x7, matrix products: 18.1 us -> 9.35 us  [layer_backward(): lax.dot_general(hidden_in, d_pre, over_rows, preferred_element_type=jnp.f...]
    dot_general x7, matrix products: 9.37 us -> 18 us  [layer_backward(): lax.dot_general(aggregate, d_pre, over_rows, preferred_element_type=jnp.f...]
  transfers between devices with their start and end apart: 29 -> 30, of which waited for: 29 -> 30; matrix products, arithmetic and copies ran while one was open for 12% -> 11% of each run, Pallas kernels for 0% -> 0%
where the time goes in v1:
time: 698 us; the launch traced here: 693 us
  waiting for transfers between devices  326 us (47%)
  starting transfers between devices  110 us (16%)
  matrix products  99.2 us (14%)
  other arithmetic  89.1 us (13%)
  local copies, waits for them, and re-layouts  53.1 us (8%)
  between operations  14.2 us (2%)
    psum x1, waiting for transfers between devices, finish_grads(): lax.psum(grad_pair[1].astype(jnp.bfloat16), 'node').astype(jnp.float32)  101 us
    all_gather x1, waiting for transfers between devices, add_all(): blocks = lax.all_gather(value, mesh_axis, axis=0, tiled=False)  73.5 us
    ppermute x14, waiting for transfers between devices, from_behind(): lax.ppermute(value, axis, [(source, source + steps) for source in range(f...  70.6 us
    all_to_all x7, waiting for transfers between devices, layer_forward(): lax.all_to_all(outgoing, 'node', split_axis=0, concat_axis=0, tiled=True)  47.2 us
    ppermute x14, starting transfers between devices, from_behind(): lax.ppermute(value, axis, [(source, source + steps) for source in range(f...  37.7 us
    all_to_all x7, starting transfers between devices, layer_forward(): lax.all_to_all(outgoing, 'node', split_axis=0, concat_axis=0, tiled=True)  36.7 us
    dynamic_update_slice x28, other arithmetic, put_row(): lax.dynamic_update_index_in_dim(buffer, jnp.where(valid, value, current),...  36.2 us
    all_to_all x7, starting transfers between devices, layer_backward(): lax.all_to_all(remote, 'node', split_axis=0, concat_axis=0, tiled=True)  35.9 us
  transfers between devices with their start and end apart: 30, of which 30 were waited for; matrix products, arithmetic and copies ran while one was open for 11% of the time, Pallas kernels for 0%

profile of v1, /device:TPU:1, one launch (start us, length us, event | category | flops | bytes accessed | tf_op | source)
XLA Modules:
  0.0 693.4 jit_solution(18045445724515416867)
XLA Ops:
  12.6 233.2 %while.44 = (s32[]{:T(128)}, bf16[256,512]{1,0:T(8,128)(2,1)S(1)}, bf16[4,256,512]{2,1,0:T(8,128)(2,1)}, bf16[4,256,512]{2,1,0:T(8,128)(2,1)}, f32[4,256,512]{2,...) while((s32[]{:T(128)}, bf16[256,512]{1,0:T(8,128)(2,1)S(1)}, ...), condition=%wide.region_1.2_spmd, body=%wide.region_0.1_spmd.sunk | while | flops 406065728 | bytes 27805224 | solution.py:172
  17.8 9.6 %all-to-all-start = ((bf16[32,8,512]{2,1,0:T(8,128)(2,1)}), bf16[32,8,512]{2,1,0:T(8,128)(2,1)S(1)}, u32[]{:S(2)}, u32[]{:S(2)}) async-start(bf16[32,8,512]{2,1,0:T(8,128)(2,1)} %fusion.105), calls=%async_computation | async-start | bytes 524288 | tf_op jit(solution)/shard_map/while/body/eval_jaxpr/all_to_all | solution.py:44
  29.7 6.6 all-to-all-done
  61.3 6.8 all-to-all-done
  94.1 6.8 all-to-all-done
  126.8 6.8 all-to-all-done
  159.6 6.8 all-to-all-done
  192.3 6.8 all-to-all-done
  225.0 6.8 all-to-all-done
  249.6 247.2 %while.45 = (s32[]{:T(128)}, bf16[256,512]{1,0:T(8,128)(2,1)}, f32[512,512]{1,0:T(8,128)}, f32[512,512]{1,0:T(8,128)}, bf16[4,256,512]{2,1,0:T(8,128)(2,1)}, /*i...) while((s32[]{:T(128)}, bf16[256,512]{1,0:T(8,128)(2,1)}, ...), condition=%wide.region_5.6_spmd.clone, body=%wide.region_3.5_spmd.clone.sunk | while | flops 700186880 | bytes 31204564 | solution.py:202
  277.7 8.1 %collective-permute-done.1 = bf16[256,512]{1,0:T(8,128)(2,1)} collective-permute-done((bf16[256,512]{1,0:T(8,128)(2,1)S(1)}, bf16[256,512]{1,0:T(8,128)(2,1)}, u32[]{:S(2)}, u32[]{:S(2)}) %collective-permute-start.1) | collective-permute-done | bytes 262176 | tf_op jit(solution)/shard_map/while/body/eval_jaxpr/ppermute | solution.py:16
  313.7 7.1 %collective-permute-done.1 = bf16[256,512]{1,0:T(8,128)(2,1)} collective-permute-done((bf16[256,512]{1,0:T(8,128)(2,1)S(1)}, bf16[256,512]{1,0:T(8,128)(2,1)}, u32[]{:S(2)}, u32[]{:S(2)}) %collective-permute-start.1) | collective-permute-done | bytes 262176 | tf_op jit(solution)/shard_map/while/body/eval_jaxpr/ppermute | solution.py:16
  328.3 5.2 all-to-all-start.1
  348.9 7.1 %collective-permute-done.1 = bf16[256,512]{1,0:T(8,128)(2,1)} collective-permute-done((bf16[256,512]{1,0:T(8,128)(2,1)S(1)}, bf16[256,512]{1,0:T(8,128)(2,1)}, u32[]{:S(2)}, u32[]{:S(2)}) %collective-permute-start.1) | collective-permute-done | bytes 262176 | tf_op jit(solution)/shard_map/while/body/eval_jaxpr/ppermute | solution.py:16
  384.1 7.1 %collective-permute-done.1 = bf16[256,512]{1,0:T(8,128)(2,1)} collective-permute-done((bf16[256,512]{1,0:T(8,128)(2,1)S(1)}, bf16[256,512]{1,0:T(8,128)(2,1)}, u32[]{:S(2)}, u32[]{:S(2)}) %collective-permute-start.1) | collective-permute-done | bytes 262176 | tf_op jit(solution)/shard_map/while/body/eval_jaxpr/ppermute | solution.py:16
  398.7 5.2 all-to-all-start.1
  419.3 7.1 %collective-permute-done.1 = bf16[256,512]{1,0:T(8,128)(2,1)} collective-permute-done((bf16[256,512]{1,0:T(8,128)(2,1)S(1)}, bf16[256,512]{1,0:T(8,128)(2,1)}, u32[]{:S(2)}, u32[]{:S(2)}) %collective-permute-start.1) | collective-permute-done | bytes 262176 | tf_op jit(solution)/shard_map/while/body/eval_jaxpr/ppermute | solution.py:16
  433.9 5.2 all-to-all-start.1
  454.5 7.1 %collective-permute-done.1 = bf16[256,512]{1,0:T(8,128)(2,1)} collective-permute-done((bf16[256,512]{1,0:T(8,128)(2,1)S(1)}, bf16[256,512]{1,0:T(8,128)(2,1)}, u32[]{:S(2)}, u32[]{:S(2)}) %collective-permute-start.1) | collective-permute-done | bytes 262176 | tf_op jit(solution)/shard_map/while/body/eval_jaxpr/ppermute | solution.py:16
  469.1 5.2 all-to-all-start.1
  489.7 7.1 %collective-permute-done.1 = bf16[256,512]{1,0:T(8,128)(2,1)} collective-permute-done((bf16[256,512]{1,0:T(8,128)(2,1)S(1)}, bf16[256,512]{1,0:T(8,128)(2,1)}, u32[]{:S(2)}, u32[]{:S(2)}) %collective-permute-start.1) | collective-permute-done | bytes 262176 | tf_op jit(solution)/shard_map/while/body/eval_jaxpr/ppermute | solution.py:16
  499.9 101.1 %all-reduce.2.cloned.1.call-done = bf16[1,512,512]{2,1,0:T(8,128)(2,1)} async-done(((bf16[1,512,512]{2,1,0:T(8,128)(2,1)}), bf16[1,512,512]{2,1,0:T(8,128)(2,1)}) %all-reduce.2.cloned.1.call-update) | async-done | bytes 524304 | tf_op jit(solution)/shard_map/psum | solution.py:116
  603.2 73.5 %all-gather.3.cloned.1.call-done = bf16[16384,512]{1,0:T(8,128)(2,1)} async-done(((bf16[512,512]{1,0:T(8,128)(2,1)}), bf16[16384,512]{1,0:T(8,128)(2,1)}) %all-gather.3.cloned.1.call-update) | async-done | bytes 16777232 | tf_op jit(solution)/shard_map/all_gather | solution.py:8
  676.6 8.8 %reduce.2 = bf16[512,512]{1,0:T(8,128)(2,1)S(1)} reduce(bf16[32,512,512]{2,1,0:T(8,128)(2,1)} %bitcast.235, bf16[]{:T(256)} %constant.228.clone.1), dimensions={0}, to_apply=%region_6.7 | reduce | flops 8126464 | bytes 17301506 | tf_op jit(solution)/shard_map/reduce_sum | solution.py:9
  (436 shorter events, 366.1 us)
Async XLA Ops:
  7.2 593.8 %all-reduce.2.cloned.1.call-start = ((), (), s32[]{:S(2)}) async-start(), calls=%async_computation.2 | async-start | bytes 1048576 | tf_op jit(solution)/shard_map/psum | solution.py:116
  17.8 18.6 %all-to-all-start = ((bf16[32,8,512]{2,1,0:T(8,128)(2,1)}), bf16[32,8,512]{2,1,0:T(8,128)(2,1)S(1)}, u32[]{:S(2)}, u32[]{:S(2)}) async-start(bf16[32,8,512]{2,1,0:T(8,128)(2,1)} %fusion.105), calls=%async_computation | async-start | bytes 524288 | tf_op jit(solution)/shard_map/while/body/eval_jaxpr/all_to_all | solution.py:44
  54.5 13.6 %all-to-all-start = ((bf16[32,8,512]{2,1,0:T(8,128)(2,1)}), bf16[32,8,512]{2,1,0:T(8,128)(2,1)S(1)}, u32[]{:S(2)}, u32[]{:S(2)}) async-start(bf16[32,8,512]{2,1,0:T(8,128)(2,1)} %fusion.105), calls=%async_computation | async-start | bytes 524288 | tf_op jit(solution)/shard_map/while/body/eval_jaxpr/all_to_all | solution.py:44
  72.3 9.7 %collective-permute-start = (bf16[256,512]{1,0:T(8,128)(2,1)S(1)}, bf16[256,512]{1,0:T(8,128)(2,1)S(1)}, u32[]{:S(2)}, u32[]{:S(2)}) collective-permute-start(bf16[256,512]{1,0:T(8,128)(2,1)S(1)} %get-tuple-element.1050), channel_id=1, source_target_pairs={{0,32},{32,64},{64,96},{1,33},{33,65},{65,97},{2,34},{34,66},{66,9... | collective-permute-start | bytes 786440 | tf_op jit(solution)/shard_map/while/body/eval_jaxpr/ppermute | solution.py:16
  87.2 13.6 %all-to-all-start = ((bf16[32,8,512]{2,1,0:T(8,128)(2,1)}), bf16[32,8,512]{2,1,0:T(8,128)(2,1)S(1)}, u32[]{:S(2)}, u32[]{:S(2)}) async-start(bf16[32,8,512]{2,1,0:T(8,128)(2,1)} %fusion.105), calls=%async_computation | async-start | bytes 524288 | tf_op jit(solution)/shard_map/while/body/eval_jaxpr/all_to_all | solution.py:44
  105.1 9.7 %collective-permute-start = (bf16[256,512]{1,0:T(8,128)(2,1)S(1)}, bf16[256,512]{1,0:T(8,128)(2,1)S(1)}, u32[]{:S(2)}, u32[]{:S(2)}) collective-permute-start(bf16[256,512]{1,0:T(8,128)(2,1)S(1)} %get-tuple-element.1050), channel_id=1, source_target_pairs={{0,32},{32,64},{64,96},{1,33},{33,65},{65,97},{2,34},{34,66},{66,9... | collective-permute-start | bytes 786440 | tf_op jit(solution)/shard_map/while/body/eval_jaxpr/ppermute | solution.py:16
  119.9 13.6 %all-to-all-start = ((bf16[32,8,512]{2,1,0:T(8,128)(2,1)}), bf16[32,8,512]{2,1,0:T(8,128)(2,1)S(1)}, u32[]{:S(2)}, u32[]{:S(2)}) async-start(bf16[32,8,512]{2,1,0:T(8,128)(2,1)} %fusion.105), calls=%async_computation | async-start | bytes 524288 | tf_op jit(solution)/shard_map/while/body/eval_jaxpr/all_to_all | solution.py:44
  137.8 9.7 %collective-permute-start = (bf16[256,512]{1,0:T(8,128)(2,1)S(1)}, bf16[256,512]{1,0:T(8,128)(2,1)S(1)}, u32[]{:S(2)}, u32[]{:S(2)}) collective-permute-start(bf16[256,512]{1,0:T(8,128)(2,1)S(1)} %get-tuple-element.1050), channel_id=1, source_target_pairs={{0,32},{32,64},{64,96},{1,33},{33,65},{65,97},{2,34},{34,66},{66,9... | collective-permute-start | bytes 786440 | tf_op jit(solution)/shard_map/while/body/eval_jaxpr/ppermute | solution.py:16
  152.7 13.6 %all-to-all-start = ((bf16[32,8,512]{2,1,0:T(8,128)(2,1)}), bf16[32,8,512]{2,1,0:T(8,128)(2,1)S(1)}, u32[]{:S(2)}, u32[]{:S(2)}) async-start(bf16[32,8,512]{2,1,0:T(8,128)(2,1)} %fusion.105), calls=%async_computation | async-start | bytes 524288 | tf_op jit(solution)/shard_map/while/body/eval_jaxpr/all_to_all | solution.py:44
  170.6 9.7 %collective-permute-start = (bf16[256,512]{1,0:T(8,128)(2,1)S(1)}, bf16[256,512]{1,0:T(8,128)(2,1)S(1)}, u32[]{:S(2)}, u32[]{:S(2)}) collective-permute-start(bf16[256,512]{1,0:T(8,128)(2,1)S(1)} %get-tuple-element.1050), channel_id=1, source_target_pairs={{0,32},{32,64},{64,96},{1,33},{33,65},{65,97},{2,34},{34,66},{66,9... | collective-permute-start | bytes 786440 | tf_op jit(solution)/shard_map/while/body/eval_jaxpr/ppermute | solution.py:16
  185.4 13.6 %all-to-all-start = ((bf16[32,8,512]{2,1,0:T(8,128)(2,1)}), bf16[32,8,512]{2,1,0:T(8,128)(2,1)S(1)}, u32[]{:S(2)}, u32[]{:S(2)}) async-start(bf16[32,8,512]{2,1,0:T(8,128)(2,1)} %fusion.105), calls=%async_computation | async-start | bytes 524288 | tf_op jit(solution)/shard_map/while/body/eval_jaxpr/all_to_all | solution.py:44
  203.3 9.7 %collective-permute-start = (bf16[256,512]{1,0:T(8,128)(2,1)S(1)}, bf16[256,512]{1,0:T(8,128)(2,1)S(1)}, u32[]{:S(2)}, u32[]{:S(2)}) collective-permute-start(bf16[256,512]{1,0:T(8,128)(2,1)S(1)} %get-tuple-element.1050), channel_id=1, source_target_pairs={{0,32},{32,64},{64,96},{1,33},{33,65},{65,97},{2,34},{34,66},{66,9... | collective-permute-start | bytes 786440 | tf_op jit(solution)/shard_map/while/body/eval_jaxpr/ppermute | solution.py:16
  218.2 13.6 %all-to-all-start = ((bf16[32,8,512]{2,1,0:T(8,128)(2,1)}), bf16[32,8,512]{2,1,0:T(8,128)(2,1)S(1)}, u32[]{:S(2)}, u32[]{:S(2)}) async-start(bf16[32,8,512]{2,1,0:T(8,128)(2,1)} %fusion.105), calls=%async_computation | async-start | bytes 524288 | tf_op jit(solution)/shard_map/while/body/eval_jaxpr/all_to_all | solution.py:44
  236.0 9.7 %collective-permute-start = (bf16[256,512]{1,0:T(8,128)(2,1)S(1)}, bf16[256,512]{1,0:T(8,128)(2,1)S(1)}, u32[]{:S(2)}, u32[]{:S(2)}) collective-permute-start(bf16[256,512]{1,0:T(8,128)(2,1)S(1)} %get-tuple-element.1050), channel_id=1, source_target_pairs={{0,32},{32,64},{64,96},{1,33},{33,65},{65,97},{2,34},{34,66},{66,9... | collective-permute-start | bytes 786440 | tf_op jit(solution)/shard_map/while/body/eval_jaxpr/ppermute | solution.py:16
  257.2 14.3 %all-to-all-start.1 = ((bf16[32,8,512]{2,1,0:T(8,128)(2,1)}), bf16[32,8,512]{2,1,0:T(8,128)(2,1)}, u32[]{:S(2)}, u32[]{:S(2)}) async-start(bf16[32,8,512]{2,1,0:T(8,128)(2,1)} %bitcast.227), calls=%async_computation.1 | async-start | bytes 524288 | tf_op jit(solution)/shard_map/while/body/eval_jaxpr/all_to_all | solution.py:101
  275.1 10.8 %collective-permute-start.1 = (bf16[256,512]{1,0:T(8,128)(2,1)S(1)}, bf16[256,512]{1,0:T(8,128)(2,1)}, u32[]{:S(2)}, u32[]{:S(2)}) collective-permute-start(bf16[256,512]{1,0:T(8,128)(2,1)S(1)} %get-tuple-element.1071), channel_id=1, source_target_pairs={{32,0},{64,32},{96,64},{33,1},{65,33},{97,65},{34,2},{66,34},{98,6... | collective-permute-start | bytes 786440 | tf_op jit(solution)/shard_map/while/body/eval_jaxpr/ppermute | solution.py:16
  293.4 14.0 %all-to-all-start.1 = ((bf16[32,8,512]{2,1,0:T(8,128)(2,1)}), bf16[32,8,512]{2,1,0:T(8,128)(2,1)}, u32[]{:S(2)}, u32[]{:S(2)}) async-start(bf16[32,8,512]{2,1,0:T(8,128)(2,1)} %bitcast.227), calls=%async_computation.1 | async-start | bytes 524288 | tf_op jit(solution)/shard_map/while/body/eval_jaxpr/all_to_all | solution.py:101
  328.3 14.3 %all-to-all-start.1 = ((bf16[32,8,512]{2,1,0:T(8,128)(2,1)}), bf16[32,8,512]{2,1,0:T(8,128)(2,1)}, u32[]{:S(2)}, u32[]{:S(2)}) async-start(bf16[32,8,512]{2,1,0:T(8,128)(2,1)} %bitcast.227), calls=%async_computation.1 | async-start | bytes 524288 | tf_op jit(solution)/shard_map/while/body/eval_jaxpr/all_to_all | solution.py:101
  346.2 9.7 %collective-permute-start.1 = (bf16[256,512]{1,0:T(8,128)(2,1)S(1)}, bf16[256,512]{1,0:T(8,128)(2,1)}, u32[]{:S(2)}, u32[]{:S(2)}) collective-permute-start(bf16[256,512]{1,0:T(8,128)(2,1)S(1)} %get-tuple-element.1071), channel_id=1, source_target_pairs={{32,0},{64,32},{96,64},{33,1},{65,33},{97,65},{34,2},{66,34},{98,6... | collective-permute-start | bytes 786440 | tf_op jit(solution)/shard_map/while/body/eval_jaxpr/ppermute | solution.py:16
  363.5 14.3 %all-to-all-start.1 = ((bf16[32,8,512]{2,1,0:T(8,128)(2,1)}), bf16[32,8,512]{2,1,0:T(8,128)(2,1)}, u32[]{:S(2)}, u32[]{:S(2)}) async-start(bf16[32,8,512]{2,1,0:T(8,128)(2,1)} %bitcast.227), calls=%async_computation.1 | async-start | bytes 524288 | tf_op jit(solution)/shard_map/while/body/eval_jaxpr/all_to_all | solution.py:101
  398.7 14.3 %all-to-all-start.1 = ((bf16[32,8,512]{2,1,0:T(8,128)(2,1)}), bf16[32,8,512]{2,1,0:T(8,128)(2,1)}, u32[]{:S(2)}, u32[]{:S(2)}) async-start(bf16[32,8,512]{2,1,0:T(8,128)(2,1)} %bitcast.227), calls=%async_computation.1 | async-start | bytes 524288 | tf_op jit(solution)/shard_map/while/body/eval_jaxpr/all_to_all | solution.py:101
  433.9 14.3 %all-to-all-start.1 = ((bf16[32,8,512]{2,1,0:T(8,128)(2,1)}), bf16[32,8,512]{2,1,0:T(8,128)(2,1)}, u32[]{:S(2)}, u32[]{:S(2)}) async-start(bf16[32,8,512]{2,1,0:T(8,128)(2,1)} %bitcast.227), calls=%async_computation.1 | async-start | bytes 524288 | tf_op jit(solution)/shard_map/while/body/eval_jaxpr/all_to_all | solution.py:101
  469.1 14.3 %all-to-all-start.1 = ((bf16[32,8,512]{2,1,0:T(8,128)(2,1)}), bf16[32,8,512]{2,1,0:T(8,128)(2,1)}, u32[]{:S(2)}, u32[]{:S(2)}) async-start(bf16[32,8,512]{2,1,0:T(8,128)(2,1)} %bitcast.227), calls=%async_computation.1 | async-start | bytes 524288 | tf_op jit(solution)/shard_map/while/body/eval_jaxpr/all_to_all | solution.py:101
  499.0 177.7 %all-gather.3.cloned.1.call-start = ((), (), s32[]{:S(2)}) async-start(), calls=%async_computation.3 | async-start | bytes 17301504 | tf_op jit(solution)/shard_map/all_gather | solution.py:8
  (48 other events, 816.3 us)
Sparse Core Ops, SparseCore 0:
  499.1 101.8 all-reduce.1
  604.1 72.4 all-gather.2
